TPU v7x, 32 devices: a whole 2x2x4 slice. The times are simulated.
32 devices in a mesh: sub: 4 (over z), row: 2 (over core), col: 4 (over y, x).
Axes of the slice: x: 2, y: 2, z: 4, core: 2. Of those that a mesh axis runs over, the one named last changes fastest.
Arguments:
- factor_cols: bfloat16 [4, 2, 2048, 4096], P('sub', None, 'col', 'row'), may hold values from -0.09375 to 0.09375
- block_pattern: int32 [4, 16, 16], P('sub'), may hold values 0 or 1
- diag_inverse: float32 [4, 4096, 2048], P('sub', ('row', 'col')), may hold values from -1 to 2
- coupling_cols: bfloat16 [4, 2, 2048, 1024], P('sub', 'row', 'col'), may hold values from -0.09375 to 0.09375
- separator_rows: int32 [4, 1024], P('sub'), may hold values from 0 to 1535, as said below
- root_inverse: float32 [1536, 1536], P('col'), may hold values from -1 to 2
- right_side: float32 [4, 4096, 128], P('sub', 'row'), may hold values from -6 to 6
- root_right: float32 [1536, 128], P('col'), may hold values from -6 to 6
Outputs:
- solution: float32 [4, 4096, 128], P('sub', ('row', 'col'))
- root_solution: float32 [1536, 128], P('col')
Inputs may be any that keep to these rules, and one draw needn't show every extreme that they name: `separator_rows`: within one section the 1024 entries are distinct.
All inputs are finite; a program needn't handle non-finite values. No bound on the sum of `block_pattern` on one device may be relied on, other than what follows from the above.
Results may differ from a plain program's by a relative error of at most 0.003.
Values may be sent and summed in bfloat16 or wider, within the bound.
A program may use at most 64 MiB of HBM per device.

v0:
```python
import functools

import jax
import jax.numpy as jnp
from jax import lax
from jax.experimental import pallas as pl
from jax.experimental.pallas import tpu as pltpu
from jax.sharding import PartitionSpec as P

BLOCK = 256
F32 = jnp.float32
BF16 = jnp.bfloat16
PIECES = 2


def mm(a, b):
    return lax.dot_general(a, b, (((1,), (0,)), ((), ())), preferred_element_type=F32)


def mm_nt(a, b):
    return lax.dot_general(a, b, (((1,), (1,)), ((), ())), preferred_element_type=F32)


def halves(x):
    high = x.astype(BF16)
    low = (x - high.astype(F32)).astype(BF16)
    return high, low


def paired(x):
    return jnp.concatenate(halves(x), axis=1)


def mm_paired(high, low, pair):
    both = mm(high, pair) + mm(low, pair)
    sources = pair.shape[1] // 2
    return both[:, :sources] + both[:, sources:]


def kernel(
    sizes,
    factor_hbm,
    pattern,
    inverse_hbm,
    couple_hbm,
    rows_ref,
    root_hbm,
    right_hbm,
    root_right,
    x_out,
    root_out,
    e_raw,
    m_raw,
    c_raw,
    r_raw,
    b_raw,
    e_hi,
    e_lo,
    et_hi,
    et_lo,
    m_mask,
    m_turn,
    spread,
    spread_turn,
    r_hi,
    r_lo,
    rt_hi,
    rt_lo,
    y_keep,
    y_low,
    y_first,
    mapped_snd,
    mapped_rcv,
    a_snd,
    a_rcv,
    a_all,
    s_snd,
    s_rcv,
    z_snd,
    z_rcv,
    rhs_hi,
    rhs_lo,
    t_snd,
    t_rcv,
    sep_low,
    root_keep,
    back_snd,
    back_rcv,
    x_all,
    give,
    take,
    load_sem,
    pair_snd,
    pair_rcv,
    col_snd,
    col_rcv,
    z_ssem,
    z_rsem,
):
    subs, cols = sizes
    sub = lax.axis_index("sub")
    row = lax.axis_index("row")
    col = lax.axis_index("col")
    width = e_raw.shape[0]
    panel = e_raw.shape[1]
    share = r_raw.shape[0]
    separator = r_raw.shape[1]

    def load(source, target, index):
        return pltpu.make_async_copy(source, target, load_sem.at[index])

    get_b = load(right_hbm.at[0], b_raw, 0)
    get_m = load(factor_hbm.at[0, 0], m_raw, 1)
    get_c = load(couple_hbm.at[0, 0], c_raw, 2)
    get_r = load(root_hbm, r_raw, 3)
    get_e = []
    for k in range(cols):
        ends = pl.ds(k * width, width)
        get_e.append(load(inverse_hbm.at[0, :, ends], e_raw.at[:, ends], 4 + k))

    @pl.when(row == 0)
    def _():
        for copy in [get_b] + get_e + [get_c]:
            copy.start()

    @pl.when(row != 0)
    def _():
        for copy in [get_m] + get_e + [get_b, get_c, get_r]:
            copy.start()

    barrier = pltpu.get_barrier_semaphore()
    pl.semaphore_signal(barrier, inc=1, device_id={"row": 1 - row})
    for d in range(1, cols):
        pl.semaphore_signal(barrier, inc=1, device_id={"col": lax.rem(col + d, cols)})
    for d in range(1, subs):
        pl.semaphore_signal(barrier, inc=1, device_id={"sub": lax.rem(sub + d, subs)})

    def ahead(d):
        return lax.rem(col + d, cols)

    def behind(d):
        return lax.rem(col + cols - d, cols)

    def part(k, size):
        return pl.ds(pl.multiple_of(k * size, size), size)

    def to_pair(source, target, index):
        return pltpu.make_async_remote_copy(
            source, target, pair_snd.at[index], pair_rcv.at[index], device_id={"row": 1 - row}
        )

    def to_col(source, target, stage, d):
        return pltpu.make_async_remote_copy(
            source, target, col_snd.at[stage, d], col_rcv.at[stage, d], device_id={"col": ahead(d)}
        )

    def rows_of(piece, size):
        return pl.ds(piece * (size // PIECES), size // PIECES)

    def piece_of(k, piece, size):
        extent = size // PIECES
        return pl.ds(pl.multiple_of(k * size + piece * extent, extent), extent)

    def scatter(make, send, receive, stage):
        size = send.shape[1]
        own, copies = [], []
        for piece in range(PIECES):
            rows = rows_of(piece, size)
            sent = []
            for d in range(1, cols):
                send[d, rows, :] = make(ahead(d), piece).astype(send.dtype)
                copy = to_col(
                    send.at[d, rows], receive.at[d, rows], stage * PIECES + piece, d
                )
                copy.start()
                sent.append(copy)
            own.append(make(col, piece))
            copies.append(sent)
        return own, copies

    def gathered(own, receive, copies, piece):
        total = own[piece]
        rows = rows_of(piece, receive.shape[1])
        for d, copy in zip(range(1, cols), copies[piece]):
            copy.wait_recv()
            total = total + receive[d, rows, :].astype(F32)
        return total

    def share_out(target, slot):
        copies = []
        for d in range(1, cols):
            copy = to_col(target, target, slot, d)
            copy.start()
            copies.append(copy)
        return copies

    def finish(copies):
        for copy in copies:
            if isinstance(copy, list):
                finish(copy)
            else:
                copy.wait_send()

    def apply_inverse():
        get_b.wait()
        total = jnp.zeros((width, b_raw.shape[1]), F32)
        for k in range(cols):
            get_e[k].wait()
            high, low = halves(e_raw[:, k * width : (k + 1) * width])
            e_hi[k] = high
            e_lo[k] = low
            pair = paired(b_raw[k * width : (k + 1) * width, :])
            total = total + mm_paired(high, low, pair)
        return total

    def turn_inverse():
        for k in range(cols):
            et_hi[k], et_lo[k] = halves(e_raw[:, k * width : (k + 1) * width].T)

    step = min(BLOCK, separator)

    def hits(first):
        at = lax.broadcasted_iota(jnp.int32, (step, rows_ref.shape[1]), 0) + first
        return jnp.where(at == rows_ref[...], 1.0, 0.0).astype(BF16)

    def make_spread():
        for first in range(0, separator, step):
            spread[first : first + step, :] = mm_nt(hits(first), c_raw[...]).astype(BF16)

    def make_spread_turn():
        for first in range(0, separator, step):
            spread_turn[:, first : first + step] = mm_nt(c_raw[...], hits(first)).astype(BF16)

    @pl.when(row == 0)
    def _():
        value = apply_inverse()
        y_keep[...] = value
        y_low[...] = value.astype(BF16)

    @pl.when(row != 0)
    def _():
        tall = min(width, BLOCK)
        get_m.wait()
        for at in range(0, width, tall):
            column = (col * width + at) // BLOCK
            for block in range(panel // BLOCK):
                present = pattern[0, panel // BLOCK + block, column].astype(F32)
                ends = slice(block * BLOCK, (block + 1) * BLOCK)
                kept = m_raw[at : at + tall, ends].astype(F32) * present
                m_raw[at : at + tall, ends] = kept.astype(BF16)
        for k in range(cols):
            piece = m_raw[:, k * width : (k + 1) * width]
            m_mask[k] = piece
            m_turn[k] = piece.astype(F32).T.astype(BF16)

    pl.semaphore_wait(barrier, 1 + (cols - 1) + (subs - 1))

    def turned(pair):
        def make(k, piece):
            rows = rows_of(piece, width)
            return mm_paired(et_hi[k, rows, :], et_lo[k, rows, :], pair)

        return make

    @pl.when(row == 0)
    def _():
        first = to_pair(y_low, y_first, 0)
        first.start()
        get_c.wait()
        make_spread()
        mapped_snd[...] = mm(spread[...], y_low[...])
        second = to_pair(mapped_snd, mapped_rcv, 1)
        second.start()
        make_spread_turn()
        turn_inverse()
        to_pair(sep_low, sep_low, 2).wait_recv()
        y_keep[...] = y_keep[...] - mm(spread_turn[...], sep_low[...])
        to_pair(root_keep, root_keep, 3).wait_recv()
        root_out[...] = root_keep[...]
        to_pair(give, take, 4).wait_recv()
        pair = paired(y_keep[...] - take[...])
        own, copies = scatter(turned(pair), back_snd, back_rcv, 7)
        for piece in range(PIECES):
            x_out[0, rows_of(piece, width), :] = gathered(own, back_rcv, copies, piece)
        finish(copies + [first, second])

    @pl.when(row != 0)
    def _():
        to_pair(y_low, y_first, 0).wait_recv()
        low = y_first[...]
        own, sends_a = scatter(
            lambda k, piece: mm(m_turn[k, rows_of(piece, width), :], low), a_snd, a_rcv, 0
        )
        started = apply_inverse()
        sends_b = []
        for piece in range(PIECES):
            rows = rows_of(piece, width)
            a_all[col, rows, :] = gathered(own, a_rcv, sends_a, piece).astype(BF16)
            sends_b.append(share_out(a_all.at[col, rows], PIECES + piece))
        get_c.wait()
        make_spread()
        value = started
        for d in range(cols):
            k = behind(d)
            if d > 0:
                for piece in range(PIECES):
                    sends_b[piece][d - 1].wait_recv()
            value = value - (mm(e_hi[k], a_all[k]) + mm(e_lo[k], a_all[k]))
        y_keep[...] = value
        own_low = value.astype(BF16)
        to_pair(mapped_snd, mapped_rcv, 1).wait_recv()

        def separator_rows(k, piece):
            rows = piece_of(k, piece, share)
            return mm(spread[rows, :], own_low) + mapped_rcv[rows, :]

        own, sends_c = scatter(separator_rows, s_snd, s_rcv, 2)
        get_r.wait()
        r_hi[...], r_lo[...] = halves(r_raw[...])
        for first in range(0, separator, step):
            ends = slice(first, first + step)
            rt_hi[ends, :], rt_lo[ends, :] = halves(r_raw[:, ends].T)
        sends_z = []
        for piece in range(PIECES):
            rows = rows_of(piece, share)
            own[piece] = gathered(own, s_rcv, sends_c, piece)
            z_snd[rows, :] = own[piece].astype(BF16)
            sent = []
            for d in range(1, subs):
                copy = pltpu.make_async_remote_copy(
                    z_snd.at[rows],
                    z_rcv.at[d, rows],
                    z_ssem.at[piece, d],
                    z_rsem.at[piece, d],
                    device_id={"sub": lax.rem(sub + d, subs)},
                )
                copy.start()
                sent.append(copy)
            sends_z.append(sent)
        make_spread_turn()
        turn_inverse()
        sends_d = []
        for piece in range(PIECES):
            rows = rows_of(piece, share)
            total = own[piece]
            for d, copy in zip(range(1, subs), sends_z[piece]):
                copy.wait_recv()
                total = total + z_rcv[d, rows, :].astype(F32)
            high, low = halves(root_right[rows, :] - total)
            place = piece_of(col, piece, share)
            rhs_hi[place, :] = high
            rhs_lo[place, :] = low
            sends_d.append(share_out(rhs_hi.at[place], 3 * PIECES + piece))
        rest = share_out(rhs_lo.at[part(col, share)], 4 * PIECES)
        for sent in sends_d:
            for copy in sent:
                copy.wait_recv()
        half = mm(r_hi[...], rhs_hi[...]) + mm(r_lo[...], rhs_hi[...])
        for copy in rest:
            copy.wait_recv()
        pair_r = paired(half + mm(r_hi[...], rhs_lo[...]))

        def root_rows(k, piece):
            rows = piece_of(k, piece, share)
            return mm_paired(rt_hi[rows, :], rt_lo[rows, :], pair_r)

        own, sends_e = scatter(root_rows, t_snd, t_rcv, 5)
        sends_f = []
        for piece in range(PIECES):
            total = gathered(own, t_rcv, sends_e, piece)
            place = piece_of(col, piece, share)
            sep_low[place, :] = total.astype(BF16)
            sends_f.append(share_out(sep_low.at[place], 6 * PIECES + piece))
            root_out[rows_of(piece, share), :] = total
            root_keep[rows_of(piece, share), :] = total
        third = to_pair(root_keep, root_keep, 3)
        third.start()
        for sent in sends_f:
            for copy in sent:
                copy.wait_recv()
        fourth = to_pair(sep_low, sep_low, 2)
        fourth.start()
        pair = paired(y_keep[...] - mm(spread_turn[...], sep_low[...]))
        own, sends_g = scatter(turned(pair), back_snd, back_rcv, 7)
        sends_h = []
        for piece in range(PIECES):
            rows = rows_of(piece, width)
            total = gathered(own, back_rcv, sends_g, piece)
            x_all[col, rows, :] = total.astype(BF16)
            sends_h.append(share_out(x_all.at[col, rows], 8 * PIECES + piece))
            x_out[0, rows, :] = total
        total = jnp.zeros(give.shape, F32)
        for d in range(cols):
            k = behind(d)
            if d > 0:
                for piece in range(PIECES):
                    sends_h[piece][d - 1].wait_recv()
            total = total + mm(m_mask[k], x_all[k])
        give[...] = total
        fifth = to_pair(give, take, 4)
        fifth.start()
        finish([sends_a, sends_b, sends_c, sends_z, sends_d, rest, sends_e, sends_f])
        finish([sends_g, sends_h, third, fourth, fifth])


def shards(
    sizes,
    factor_cols,
    block_pattern,
    diag_inverse,
    coupling_cols,
    separator_rows,
    root_inverse,
    right_side,
    root_right,
):
    subs, cols = sizes
    width, panel = diag_inverse.shape[1:]
    share, separator = root_inverse.shape
    sources = right_side.shape[2]
    coupled = coupling_cols.shape[3]
    hbm = pl.BlockSpec(memory_space=pl.ANY)
    vmem = pl.BlockSpec(memory_space=pltpu.VMEM)
    smem = pl.BlockSpec(memory_space=pltpu.SMEM)
    V = pltpu.VMEM
    tile = (cols, width, width)
    scratch = [
        V((width, panel), F32),
        V((width, panel), BF16),
        V((width, coupled), BF16),
        V((share, separator), F32),
        V((panel, sources), F32),
        V(tile, BF16),
        V(tile, BF16),
        V(tile, BF16),
        V(tile, BF16),
        V(tile, BF16),
        V(tile, BF16),
        V((separator, width), BF16),
        V((width, separator), BF16),
        V((share, separator), BF16),
        V((share, separator), BF16),
        V((separator, share), BF16),
        V((separator, share), BF16),
        V((width, sources), F32),
        V((width, sources), BF16),
        V((width, sources), BF16),
        V((separator, sources), F32),
        V((separator, sources), F32),
        V((cols, width, sources), BF16),
        V((cols, width, sources), BF16),
        V((cols, width, sources), BF16),
        V((cols, share, sources), BF16),
        V((cols, share, sources), BF16),
        V((share, sources), BF16),
        V((subs, share, sources), BF16),
        V((separator, sources), BF16),
        V((separator, sources), BF16),
        V((cols, share, sources), BF16),
        V((cols, share, sources), BF16),
        V((separator, sources), BF16),
        V((share, sources), F32),
        V((cols, width, sources), BF16),
        V((cols, width, sources), BF16),
        V((cols, width, sources), BF16),
        V((width, sources), F32),
        V((width, sources), F32),
        pltpu.SemaphoreType.DMA((4 + cols,)),
        pltpu.SemaphoreType.DMA((5,)),
        pltpu.SemaphoreType.DMA((5,)),
        pltpu.SemaphoreType.DMA((10 * PIECES, cols)),
        pltpu.SemaphoreType.DMA((10 * PIECES, cols)),
        pltpu.SemaphoreType.DMA((PIECES, subs)),
        pltpu.SemaphoreType.DMA((PIECES, subs)),
    ]
    return pl.pallas_call(
        functools.partial(kernel, sizes),
        out_shape=(
            jax.ShapeDtypeStruct((1, width, sources), F32),
            jax.ShapeDtypeStruct((share, sources), F32),
        ),
        in_specs=[hbm, smem, hbm, hbm, vmem, hbm, hbm, vmem],
        out_specs=(vmem, vmem),
        scratch_shapes=scratch,
        compiler_params=pltpu.CompilerParams(
            collective_id=0, has_side_effects=True, vmem_limit_bytes=60 * 1024 * 1024
        ),
        name="tree_solve",
    )(
        factor_cols,
        block_pattern,
        diag_inverse,
        coupling_cols,
        separator_rows,
        root_inverse,
        right_side,
        root_right,
    )


def solution(mesh):
    sizes = (mesh.shape["sub"], mesh.shape["col"])
    return jax.shard_map(
        functools.partial(shards, sizes),
        mesh=mesh,
        in_specs=(
            P("sub", None, "col", "row"),
            P("sub", None, None),
            P("sub", ("row", "col"), None),
            P("sub", "row", "col", None),
            P("sub", None),
            P("col", None),
            P("sub", "row", None),
            P("col", None),
        ),
        out_specs=(P("sub", ("row", "col"), None), P("col", None)),
        check_vma=False,
    )
```

profile of v0, /device:TPU:0, one launch (start us, length us, event | category | flops | bytes accessed | tf_op | source)
XLA Modules:
  0.0 66.9 jit_solution(3016005085684765789)
XLA Ops:
  0.6 62.9 %tree_solve.1 = (f32[1,512,128]{2,1,0:T(8,128)}, f32[384,128]{1,0:T(8,128)}) custom-call(bf16[1,2,512,2048]{3,2,1,0:T(8,128)(2,1)} %factor_hbm.1, s32[1,16,16]{2,1,0:T(8,128)} %pattern.1, f32[1,512,2048]{2,1,0:T(8,128)} %inverse_hbm.1, bf16[1,1,512,1024]{3,2,1,0:T(8,128)(2,1)} %couple_hbm.1, s32[1,1024]{1,0:T(1,128)} %rows_ref.1, f32[384,1536]{1,0:T(8,128)} %root_hbm.1, ...), custom_call_target="tpu_custom_call" | custom-call | tf_op jit(solution)/shard_map/tree_solve/pallas_call | solution.py:476
  63.6 1.7 %copy.12 = f32[1,512,128]{2,1,0:T(8,128)} copy(f32[1,512,128]{2,1,0:T(8,128)} %get-tuple-element.4) | data formatting | bytes 524288
  65.2 1.6 %copy.13 = f32[384,128]{1,0:T(8,128)} copy(f32[384,128]{1,0:T(8,128)} %get-tuple-element.5) | data formatting | bytes 393216
where the time goes:
time: 67.1 us; the launch traced here: 66.9 us
  Pallas kernels  62.9 us (94%)
  local copies, waits for them, and re-layouts  3.29 us (5%)
    pallas_call x1, Pallas kernels, shards(): pl.pallas_call(functools.partial(kernel, sizes), out_shape=(jax.ShapeDtyp...  62.9 us
    unnamed x2, local copies, waits for them, and re-layouts  3.29 us

commit v1 on v0

--- a/solution.py
+++ b/solution.py
@@ -40,13 +40,13 @@
 def kernel(
     sizes,
     factor_hbm,
-    pattern,
+    pattern_hbm,
     inverse_hbm,
     couple_hbm,
-    rows_ref,
+    rows_hbm,
     root_hbm,
     right_hbm,
-    root_right,
+    root_right_hbm,
     x_out,
     root_out,
     e_raw,
@@ -96,6 +96,9 @@
     col_rcv,
     z_ssem,
     z_rsem,
+    pattern,
+    rows_ref,
+    root_right,
 ):
     subs, cols = sizes
     sub = lax.axis_index("sub")
@@ -113,6 +116,9 @@
     get_m = load(factor_hbm.at[0, 0], m_raw, 1)
     get_c = load(couple_hbm.at[0, 0], c_raw, 2)
     get_r = load(root_hbm, r_raw, 3)
+    get_p = load(pattern_hbm, pattern, 4 + cols)
+    get_n = load(rows_hbm, rows_ref, 5 + cols)
+    get_rr = load(root_right_hbm, root_right, 6 + cols)
     get_e = []
     for k in range(cols):
         ends = pl.ds(k * width, width)
@@ -120,12 +126,12 @@
 
     @pl.when(row == 0)
     def _():
-        for copy in [get_b] + get_e + [get_c]:
+        for copy in [get_b] + get_e + [get_n, get_c]:
             copy.start()
 
     @pl.when(row != 0)
     def _():
-        for copy in [get_m] + get_e + [get_b, get_c, get_r]:
+        for copy in [get_p, get_m, get_n] + get_e + [get_b, get_c, get_r, get_rr]:
             copy.start()
 
     barrier = pltpu.get_barrier_semaphore()
@@ -240,6 +246,7 @@
     @pl.when(row != 0)
     def _():
         tall = min(width, BLOCK)
+        get_p.wait()
         get_m.wait()
         for at in range(0, width, tall):
             column = (col * width + at) // BLOCK
@@ -267,6 +274,7 @@
         first = to_pair(y_low, y_first, 0)
         first.start()
         get_c.wait()
+        get_n.wait()
         make_spread()
         mapped_snd[...] = mm(spread[...], y_low[...])
         second = to_pair(mapped_snd, mapped_rcv, 1)
@@ -298,6 +306,7 @@
             a_all[col, rows, :] = gathered(own, a_rcv, sends_a, piece).astype(BF16)
             sends_b.append(share_out(a_all.at[col, rows], PIECES + piece))
         get_c.wait()
+        get_n.wait()
         make_spread()
         value = started
         for d in range(cols):
@@ -316,6 +325,7 @@
 
         own, sends_c = scatter(separator_rows, s_snd, s_rcv, 2)
         get_r.wait()
+        get_rr.wait()
         r_hi[...], r_lo[...] = halves(r_raw[...])
         for first in range(0, separator, step):
             ends = slice(first, first + step)
@@ -419,7 +429,7 @@
     share, separator = root_inverse.shape
     sources = right_side.shape[2]
     coupled = coupling_cols.shape[3]
-    hbm = pl.BlockSpec(memory_space=pl.ANY)
+    hbm = pl.BlockSpec(memory_space=pltpu.HBM)
     vmem = pl.BlockSpec(memory_space=pltpu.VMEM)
     smem = pl.BlockSpec(memory_space=pltpu.SMEM)
     V = pltpu.VMEM
@@ -465,28 +475,31 @@
         V((cols, width, sources), BF16),
         V((width, sources), F32),
         V((width, sources), F32),
-        pltpu.SemaphoreType.DMA((4 + cols,)),
+        pltpu.SemaphoreType.DMA((7 + cols,)),
         pltpu.SemaphoreType.DMA((5,)),
         pltpu.SemaphoreType.DMA((5,)),
         pltpu.SemaphoreType.DMA((10 * PIECES, cols)),
         pltpu.SemaphoreType.DMA((10 * PIECES, cols)),
         pltpu.SemaphoreType.DMA((PIECES, subs)),
         pltpu.SemaphoreType.DMA((PIECES, subs)),
+        pltpu.SMEM(block_pattern.shape, jnp.int32),
+        V(separator_rows.shape, jnp.int32),
+        V(root_right.shape, F32),
     ]
-    return pl.pallas_call(
+    x, root = pl.pallas_call(
         functools.partial(kernel, sizes),
         out_shape=(
             jax.ShapeDtypeStruct((1, width, sources), F32),
             jax.ShapeDtypeStruct((share, sources), F32),
         ),
-        in_specs=[hbm, smem, hbm, hbm, vmem, hbm, hbm, vmem],
+        in_specs=[hbm] * 8,
         out_specs=(vmem, vmem),
         scratch_shapes=scratch,
         compiler_params=pltpu.CompilerParams(
-            collective_id=0, has_side_effects=True, vmem_limit_bytes=60 * 1024 * 1024
+            collective_id=0, has_side_effects=True, vmem_limit_bytes=52 * 1024 * 1024
         ),
         name="tree_solve",
-    )(
+    )(*[pltpu.with_memory_space_constraint(v, pltpu.HBM) for v in (
         factor_cols,
         block_pattern,
         diag_inverse,
@@ -495,7 +508,27 @@
         root_inverse,
         right_side,
         root_right,
-    )
+    )])
+    return pl.pallas_call(
+        publish,
+        out_shape=(
+            jax.ShapeDtypeStruct((1, width, sources), F32),
+            jax.ShapeDtypeStruct((share, sources), F32),
+        ),
+        in_specs=[vmem, vmem],
+        out_specs=(hbm, hbm),
+        scratch_shapes=[pltpu.SemaphoreType.DMA((2,))],
+        compiler_params=pltpu.CompilerParams(vmem_limit_bytes=2 * 1024 * 1024),
+        name="publish",
+    )(x, root)
+
+
+def publish(x, root, x_out, root_out, sem):
+    outs = [pltpu.make_async_copy(x, x_out, sem.at[0]), pltpu.make_async_copy(root, root_out, sem.at[1])]
+    for out in outs:
+        out.start()
+    for out in outs:
+        out.wait()
 
 
 def solution(mesh):

time: 67.1 us -> 63 us (0.939)
  local copies, waits for them, and re-layouts: 3.29 us -> 0 us
  Pallas kernels: 62.9 us -> 62 us
    unnamed x2 -> x0, local copies, waits for them, and re-layouts: 3.29 us -> none
    pallas_call x1, Pallas kernels: 62.9 us -> 61.2 us  [shards(): pl.pallas_call(functools.partial(kernel, sizes), out_shape=(jax.ShapeDtyp...]
    pallas_call x0 -> x1, Pallas kernels: none -> 0.78 us  [shards(): pl.pallas_call(publish, out_shape=(jax.ShapeDtypeStruct((1, width, source...]
where the time goes in v1:
time: 63 us; the launch traced here: 62.8 us
  Pallas kernels  62 us (98%)
  between operations  0.82 us (1%)
    pallas_call x1, Pallas kernels, shards(): pl.pallas_call(functools.partial(kernel, sizes), out_shape=(jax.ShapeDtyp...  61.2 us

profile of v1, /device:TPU:0, one launch (start us, length us, event | category | flops | bytes accessed | tf_op | source)
XLA Modules:
  0.0 62.8 jit_solution(15049833723968920802)
XLA Ops:
  0.6 61.2 %tree_solve.1 = (f32[1,512,128]{2,1,0:T(8,128)S(1)}, f32[384,128]{1,0:T(8,128)S(1)}) custom-call(bf16[1,2,512,2048]{3,2,1,0:T(8,128)(2,1)} %factor_hbm.1, s32[1,16,16]{2,1,0:T(8,128)} %pattern_hbm.1, f32[1,512,2048]{2,1,0:T(8,128)} %inverse_hbm.1, bf16[1,1,512,1024]{3,2,1,0:T(8,128)(2,1)} %couple_hbm.1, s32[1,1024]{1,0:T(1,128)} %rows_hbm.1, ...), custom_call_target="tpu_custom_call" | custom-call | tf_op jit(solution)/shard_map/tree_solve/pallas_call | solution.py:489
  61.9 0.8 %publish.1 = (f32[1,512,128]{2,1,0:T(8,128)}, f32[384,128]{1,0:T(8,128)}) custom-call(f32[1,512,128]{2,1,0:T(8,128)S(1)} %get-tuple-element.4.x, f32[384,128]{1,0:T(8,128)S(1)} %get-tuple-element.5.root), custom_call_target="tpu_custom_call" | custom-call | tf_op jit(solution)/shard_map/publish/pallas_call | solution.py:512

commit v2 on v1

v2 whole, which is shorter than its diff:
```python
import functools

import jax
import jax.numpy as jnp
from jax import lax
from jax.experimental import pallas as pl
from jax.experimental.pallas import tpu as pltpu
from jax.sharding import PartitionSpec as P

BLOCK = 256
F32 = jnp.float32
BF16 = jnp.bfloat16
CHUNKS = 2
SLOTS = 4


def mm(a, b):
    return lax.dot_general(a, b, (((1,), (0,)), ((), ())), preferred_element_type=F32)


def mm_nt(a, b):
    return lax.dot_general(a, b, (((1,), (1,)), ((), ())), preferred_element_type=F32)


def halves(x):
    high = x.astype(BF16)
    low = (x - high.astype(F32)).astype(BF16)
    return high, low


def paired(x):
    return jnp.concatenate(halves(x), axis=1)


def mm_paired(high, low, pair):
    both = mm(high, pair) + mm(low, pair)
    sources = pair.shape[1] // 2
    return both[:, :sources] + both[:, sources:]


def divided(size, most):
    count = most
    while count > 1 and size % (16 * count):
        count //= 2
    return count


def offsets(cols):
    tall = max(s for s in range(1, cols + 1) if s * s <= cols and cols % s == 0)
    wide = cols // tall
    steps = [(y, x) for y in range(tall) for x in range(wide)]

    def hops(step):
        return min(step[0], tall - step[0]) + min(step[1], wide - step[1])

    far = sorted(steps[1:], key=lambda step: (-hops(step), -step[0], -step[1]))
    return tall, wide, [(0, 0)] + far


def kernel(
    sizes,
    factor_hbm,
    pattern_hbm,
    inverse_hbm,
    couple_hbm,
    rows_hbm,
    root_hbm,
    right_hbm,
    root_right_hbm,
    x_out,
    root_out,
    e_raw,
    m_raw,
    c_raw,
    r_raw,
    b_raw,
    b_pair,
    w_pair,
    e_hi,
    e_lo,
    et_hi,
    et_lo,
    m_turn,
    spread,
    spread_turn,
    r_hi,
    r_lo,
    rt_hi,
    rt_lo,
    y_keep,
    y_low,
    mapped_snd,
    mapped_rcv,
    part_own,
    part_snd,
    a_rcv,
    a_all,
    s_rcv,
    z_snd,
    z_rcv,
    rhs_hi,
    rhs_lo,
    t_rcv,
    sep_low,
    root_keep,
    back_rcv,
    x_all,
    pattern,
    rows_ref,
    root_right,
    load_sem,
    pair_snd,
    pair_rcv,
    col_snd,
    col_rcv,
    z_ssem,
    z_rsem,
):
    subs, cols = sizes
    sub = lax.axis_index("sub")
    row = lax.axis_index("row")
    col = lax.axis_index("col")
    width = e_raw.shape[0]
    panel = e_raw.shape[1]
    share = r_raw.shape[0]
    separator = r_raw.shape[1]
    tall, wide, steps = offsets(cols)
    col_y = lax.div(col, wide)
    col_x = lax.rem(col, wide)

    def ahead(i):
        y, x = steps[i]
        return lax.rem(col_y + y, tall) * wide + lax.rem(col_x + x, wide)

    def behind(i):
        y, x = steps[i]
        return lax.rem(col_y + (tall - y), tall) * wide + lax.rem(col_x + (wide - x), wide)

    def load(source, target, index):
        return pltpu.make_async_copy(source, target, load_sem.at[index])

    thick = width // CHUNKS
    get_b = load(right_hbm.at[0], b_raw, 0)
    get_m = load(factor_hbm.at[0, 0], m_raw, 1)
    get_c = load(couple_hbm.at[0, 0], c_raw, 2)
    get_r = load(root_hbm, r_raw, 3)
    get_p = load(pattern_hbm, pattern, 4)
    get_n = load(rows_hbm, rows_ref, 5)
    get_rr = load(root_right_hbm, root_right, 6)
    get_e = []
    for c in range(CHUNKS):
        rows = pl.ds(c * thick, thick)
        get_e.append(load(inverse_hbm.at[0, rows], e_raw.at[rows], 7 + c))

    @pl.when(row == 0)
    def _():
        for copy in [get_b] + get_e + [get_n, get_c]:
            copy.start()

    @pl.when(row != 0)
    def _():
        for copy in [get_p, get_m, get_n, get_c, get_b] + get_e + [get_r, get_rr]:
            copy.start()

    barrier = pltpu.get_barrier_semaphore()
    pl.semaphore_signal(barrier, inc=1, device_id={"row": 1 - row})
    for i in range(1, cols):
        pl.semaphore_signal(barrier, inc=1, device_id={"col": ahead(i)})
        pl.semaphore_signal(barrier, inc=1, device_id={"row": 1 - row, "col": ahead(i)})
    for d in range(1, subs):
        pl.semaphore_signal(barrier, inc=1, device_id={"sub": lax.rem(sub + d, subs)})

    def greet():
        pl.semaphore_wait(barrier, 1 + 2 * (cols - 1) + (subs - 1))

    def part(k, size):
        return pl.ds(pl.multiple_of(k * size, size), size)

    def to_pair(source, target, index):
        return pltpu.make_async_remote_copy(
            source, target, pair_snd.at[index], pair_rcv.at[index], device_id={"row": 1 - row}
        )

    def to_col(source, target, slot, i):
        return pltpu.make_async_remote_copy(
            source, target, col_snd.at[slot // SLOTS], col_rcv.at[slot, i], device_id={"col": ahead(i)}
        )

    def to_other(source, target, slot, i):
        return pltpu.make_async_remote_copy(
            source,
            target,
            col_snd.at[slot // SLOTS],
            col_rcv.at[slot, i],
            device_id={"row": 1 - row, "col": ahead(i)},
        )

    def scatter(make, size, receive, segments, pieces):
        pieces = divided(size, pieces)
        segments = min(segments, pieces)
        extent = size // segments
        fine = size // pieces
        copies = []
        for segment in range(segments):
            rows = pl.ds(segment * extent, extent)
            for i in range(1, cols):
                value = make(i, ahead(i), segment * extent, extent)
                part_snd[i, rows, :] = value.astype(BF16)
            part_own[rows, :] = make(0, col, segment * extent, extent)
            for piece in range(pieces // segments):
                at = pl.ds(segment * extent + piece * fine, fine)
                slot = len(copies)
                sent = []
                for i in range(1, cols):
                    copy = to_col(part_snd.at[i, at], receive.at[i, at], slot, i)
                    copy.start()
                    sent.append(copy)
                copies.append((at, sent))
        return copies

    def gathered(receive, at, sent):
        for copy in sent:
            copy.wait_recv()
        total = part_own[at, :]
        for i in range(1, cols):
            total = total + receive[i, at, :].astype(F32)
        return total

    def share_out(target, slot):
        copies = []
        for i in range(1, cols):
            copy = to_col(target, target, slot, i)
            copy.start()
            copies.append(copy)
        return copies

    def sent_out(kind, first, size):
        block = part_snd.at[pl.ds(first, cols - first), pl.ds(0, size)]
        pltpu.make_async_remote_copy(
            block, block, col_snd.at[kind], col_rcv.at[0, 0], device_id={"row": 1 - row}
        ).wait_send()

    def sent_across():
        block = z_rcv.at[pl.ds(1, subs - 1)]
        pltpu.make_async_remote_copy(
            block, block, z_ssem.at[0], z_rsem.at[0, 0], device_id={"row": 1 - row}
        ).wait_send()

    def finish(copies):
        for copy in copies:
            copy.wait_send()

    def apply_inverse(c, put):
        rows = pl.ds(c * thick, thick)
        high, low = halves(e_raw[rows, :])
        e_hi[rows, :] = high
        e_lo[rows, :] = low
        put(rows, mm_paired(high, low, b_pair[...]))

    def turn_inverse():
        for i in range(cols):
            block = e_raw[:, part(ahead(i), width)]
            et_hi[i], et_lo[i] = halves(block.T)

    step = min(BLOCK, separator)

    def hits(first):
        at = lax.broadcasted_iota(jnp.int32, (step, rows_ref.shape[1]), 0) + first
        return jnp.where(at == rows_ref[...], 1.0, 0.0).astype(BF16)

    def make_spread():
        for first in range(0, separator, step):
            spread[first : first + step, :] = mm_nt(hits(first), c_raw[...]).astype(BF16)

    def make_spread_turn():
        for first in range(0, separator, step):
            spread_turn[:, first : first + step] = mm_nt(c_raw[...], hits(first)).astype(BF16)

    def turned(i, k, start, extent):
        rows = pl.ds(start, extent)
        return mm_paired(et_hi[i, rows, :], et_lo[i, rows, :], w_pair[0:width, :])

    y_parts = []
    for c in range(CHUNKS):
        rows = pl.ds(c * thick, thick)
        y_parts.append(to_pair(y_low.at[rows], y_low.at[rows], 4 + c))
    m_whole = to_pair(m_raw, m_raw, 0)
    mapped_whole = to_pair(mapped_snd, mapped_rcv, 1)
    sep_whole = to_pair(sep_low, sep_low, 2)
    root_whole = to_pair(root_keep, root_keep, 3)

    @pl.when(row == 0)
    def _():
        def put(rows, value):
            y_keep[rows, :] = value
            y_low[rows, :] = value.astype(BF16)

        get_b.wait()
        b_pair[...] = paired(b_raw[...])
        for c in range(CHUNKS):
            get_e[c].wait()
            apply_inverse(c, put)
            if c == 0:
                greet()
            y_parts[c].start()
        get_c.wait()
        get_n.wait()
        make_spread()
        mapped_snd[...] = mm(spread[...], y_low[...])
        mapped_whole.start()
        make_spread_turn()
        turn_inverse()
        sep_whole.wait_recv()
        y_keep[...] = y_keep[...] - mm(spread_turn[...], sep_low[...])
        root_whole.wait_recv()
        root_out[...] = root_keep[...]
        m_whole.wait_recv()
        count = divided(width, 4)
        fine = width // count
        near = [0] + list(range(2, cols))
        for group in (near, [1]):
            for i in group:
                for piece in range(count):
                    at = pl.ds(piece * fine, fine)
                    to_other(
                        x_all.at[i, at], x_all.at[i, at], SLOTS + piece, i
                    ).wait_recv()
            total = y_keep[...]
            for i in group:
                total = total - mm(m_raw[:, part(behind(i), width)], x_all[i])
            if group is near:
                y_keep[...] = total
            else:
                w_pair[0:width, :] = paired(total)
        sends = scatter(turned, width, back_rcv, 2, 4)
        for at, sent in sends:
            x_out[0, at, :] = gathered(back_rcv, at, sent)
        sent_out(0, 1, width)
        finish(y_parts + [mapped_whole])

    @pl.when(row != 0)
    def _():
        high_rows = min(width, BLOCK)
        get_p.wait()
        get_m.wait()
        for at in range(0, width, high_rows):
            column = lax.div(col * width + at, BLOCK)
            for block in range(panel // BLOCK):
                present = pattern[0, panel // BLOCK + block, column].astype(F32)
                ends = slice(block * BLOCK, (block + 1) * BLOCK)
                kept = m_raw[at : at + high_rows, ends].astype(F32) * present
                m_raw[at : at + high_rows, ends] = kept.astype(BF16)
        greet()
        m_whole.start()
        for i in range(cols):
            block = m_raw[:, part(ahead(i), width)]
            m_turn[i] = block.astype(F32).T.astype(BF16)
        rhs_lo[...] = jnp.zeros(rhs_lo.shape, BF16)
        get_c.wait()
        get_n.wait()
        make_spread()
        for copy in y_parts:
            copy.wait_recv()

        def a_rows(i, k, start, extent):
            return mm(m_turn[i, pl.ds(start, extent), :], y_low[...])

        sends_a = scatter(a_rows, width, a_rcv, 2, 4)

        def put(rows, value):
            y_keep[rows, :] = value

        get_b.wait()
        b_pair[...] = paired(b_raw[...])
        for copy in get_e:
            copy.wait()
        for c in range(CHUNKS):
            apply_inverse(c, put)
        sends_b = []
        for at, sent in sends_a:
            a_all[col, at, :] = gathered(a_rcv, at, sent).astype(BF16)
            sends_b.append(share_out(a_all.at[col, at], SLOTS + len(sends_b)))
        make_spread_turn()
        for group in ([0] + list(range(2, cols)), [1]):
            for i in group:
                if i > 0:
                    for sent in sends_b:
                        sent[i - 1].wait_recv()
            total = y_keep[...]
            for i in group:
                k = behind(i)
                ends = part(k, width)
                total = total - (mm(e_hi[:, ends], a_all[k]) + mm(e_lo[:, ends], a_all[k]))
            y_keep[...] = total
        y_low[...] = y_keep[...].astype(BF16)
        mapped_whole.wait_recv()

        def separator_rows(i, k, start, extent):
            place = pl.ds(pl.multiple_of(k * share + start, 16), extent)
            return mm(spread[place, :], y_low[...]) + mapped_rcv[place, :]

        sent_out(0, 1, width)
        sends_c = scatter(separator_rows, share, s_rcv, 2, 4)
        get_r.wait()
        get_rr.wait()
        r_hi[...], r_lo[...] = halves(r_raw[...])
        for first in range(0, separator, step):
            ends = slice(first, first + step)
            rt_hi[ends, :], rt_lo[ends, :] = halves(r_raw[:, ends].T)
        sends_z = []
        for piece, (at, sent) in enumerate(sends_c):
            total = gathered(s_rcv, at, sent)
            part_own[at, :] = total
            z_snd[at, :] = total.astype(BF16)
            copies = []
            for d in range(1, subs):
                copy = pltpu.make_async_remote_copy(
                    z_snd.at[at],
                    z_rcv.at[d, at],
                    z_ssem.at[0],
                    z_rsem.at[piece, d - 1],
                    device_id={"sub": lax.rem(sub + d, subs)},
                )
                copy.start()
                copies.append(copy)
            sends_z.append((at, copies))
        turn_inverse()
        sent_out(1, 1, width)
        sends_d = []
        fine = share // len(sends_z)
        for piece, (at, copies) in enumerate(sends_z):
            for copy in copies:
                copy.wait_recv()
            total = part_own[at, :]
            for d in range(1, subs):
                total = total + z_rcv[d, at, :].astype(F32)
            high, low = halves(root_right[at, :] - total)
            place = pl.ds(pl.multiple_of(col * share + piece * fine, 16), fine)
            rhs_hi[place, :] = high
            rhs_lo[place, :] = low
            sends_d.append(share_out(rhs_hi.at[place], SLOTS + piece))
        own_half = mm(r_hi[...], rhs_lo[...])
        part_own[0:share, :] = own_half
        for sent in sends_d:
            for copy in sent:
                copy.wait_recv()
        half = mm(r_hi[...], rhs_hi[...]) + mm(r_lo[...], rhs_hi[...])
        w_pair[0:share, :] = paired(half + part_own[0:share, :])

        def root_rows(i, k, start, extent):
            place = pl.ds(pl.multiple_of(k * share + start, 16), extent)
            return mm_paired(rt_hi[place, :], rt_lo[place, :], w_pair[0:share, :])

        sent_out(0, 1, share)
        sends_e = scatter(root_rows, share, t_rcv, 2, 2)
        sent_out(1, 1, share)
        sends_f = []
        fine = share // len(sends_e)
        for piece, (at, sent) in enumerate(sends_e):
            total = gathered(t_rcv, at, sent)
            place = pl.ds(pl.multiple_of(col * share + piece * fine, 16), fine)
            sep_low[place, :] = total.astype(BF16)
            sends_f.append(share_out(sep_low.at[place], SLOTS + piece))
            root_out[at, :] = total
            root_keep[at, :] = total
        root_whole.start()
        for sent in sends_f:
            for copy in sent:
                copy.wait_recv()
        sep_whole.start()
        w_pair[0:width, :] = paired(y_keep[...] - mm(spread_turn[...], sep_low[...]))
        sent_out(0, 1, share)
        sends_g = scatter(turned, width, back_rcv, 2, 4)
        sent_out(1, 1, share)
        for piece, (at, sent) in enumerate(sends_g):
            total = gathered(back_rcv, at, sent)
            y_low[at, :] = total.astype(BF16)
            for i in list(range(1, cols)) + [0]:
                copy = to_other(y_low.at[at], x_all.at[i, at], SLOTS + piece, i)
                copy.start()
            x_out[0, at, :] = total
        sent_across()
        sent_out(0, 1, width)
        sent_out(1, 0, width)
        finish([m_whole, root_whole, sep_whole])


def publish(x, root, x_out, root_out, sem):
    copies = [
        pltpu.make_async_copy(x, x_out, sem.at[0]),
        pltpu.make_async_copy(root, root_out, sem.at[1]),
    ]
    for copy in copies:
        copy.start()
    for copy in copies:
        copy.wait()


def shards(
    sizes,
    factor_cols,
    block_pattern,
    diag_inverse,
    coupling_cols,
    separator_rows,
    root_inverse,
    right_side,
    root_right,
):
    subs, cols = sizes
    width, panel = diag_inverse.shape[1:]
    share, separator = root_inverse.shape
    sources = right_side.shape[2]
    coupled = coupling_cols.shape[3]
    hbm = pl.BlockSpec(memory_space=pltpu.HBM)
    vmem = pl.BlockSpec(memory_space=pltpu.VMEM)
    V = pltpu.VMEM
    DMA = pltpu.SemaphoreType.DMA
    tile = (cols, width, width)
    most = max(width, share)
    scratch = [
        V((width, panel), F32),
        V((width, panel), BF16),
        V((width, coupled), BF16),
        V((share, separator), F32),
        V((panel, sources), F32),
        V((panel, 2 * sources), BF16),
        V((most, 2 * sources), BF16),
        V((width, panel), BF16),
        V((width, panel), BF16),
        V(tile, BF16),
        V(tile, BF16),
        V(tile, BF16),
        V((separator, width), BF16),
        V((width, separator), BF16),
        V((share, separator), BF16),
        V((share, separator), BF16),
        V((separator, share), BF16),
        V((separator, share), BF16),
        V((width, sources), F32),
        V((width, sources), BF16),
        V((separator, sources), F32),
        V((separator, sources), F32),
        V((most, sources), F32),
        V((cols, most, sources), BF16),
        V((cols, width, sources), BF16),
        V((cols, width, sources), BF16),
        V((cols, share, sources), BF16),
        V((share, sources), BF16),
        V((subs, share, sources), BF16),
        V((separator, sources), BF16),
        V((separator, sources), BF16),
        V((cols, share, sources), BF16),
        V((separator, sources), BF16),
        V((share, sources), F32),
        V((cols, width, sources), BF16),
        V((cols, width, sources), BF16),
        pltpu.SMEM(block_pattern.shape, jnp.int32),
        V(separator_rows.shape, jnp.int32),
        V(root_right.shape, F32),
        DMA((7 + CHUNKS,)),
        DMA((4 + CHUNKS,)),
        DMA((4 + CHUNKS,)),
        DMA((2,)),
        DMA((2 * SLOTS, cols)),
        DMA((1,)),
        DMA((SLOTS, subs - 1)),
    ]
    inputs = (
        factor_cols,
        block_pattern,
        diag_inverse,
        coupling_cols,
        separator_rows,
        root_inverse,
        right_side,
        root_right,
    )
    shapes = (
        jax.ShapeDtypeStruct((1, width, sources), F32),
        jax.ShapeDtypeStruct((share, sources), F32),
    )
    x, root = pl.pallas_call(
        functools.partial(kernel, sizes),
        out_shape=shapes,
        in_specs=[hbm] * 8,
        out_specs=(vmem, vmem),
        scratch_shapes=scratch,
        compiler_params=pltpu.CompilerParams(
            collective_id=0, has_side_effects=True, vmem_limit_bytes=52 * 1024 * 1024
        ),
        name="tree_solve",
    )(*[pltpu.with_memory_space_constraint(value, pltpu.HBM) for value in inputs])
    return pl.pallas_call(
        publish,
        out_shape=shapes,
        in_specs=[vmem, vmem],
        out_specs=(hbm, hbm),
        scratch_shapes=[DMA((2,))],
        compiler_params=pltpu.CompilerParams(vmem_limit_bytes=2 * 1024 * 1024),
        name="publish",
    )(x, root)


def solution(mesh):
    sizes = (mesh.shape["sub"], mesh.shape["col"])
    return jax.shard_map(
        functools.partial(shards, sizes),
        mesh=mesh,
        in_specs=(
            P("sub", None, "col", "row"),
            P("sub", None, None),
            P("sub", ("row", "col"), None),
            P("sub", "row", "col", None),
            P("sub", None),
            P("col", None),
            P("sub", "row", None),
            P("col", None),
        ),
        out_specs=(P("sub", ("row", "col"), None), P("col", None)),
        check_vma=False,
    )
```

time: 63 us -> 58.4 us (0.927)
  Pallas kernels: 62 us -> 57.5 us
    pallas_call x2, Pallas kernels: 62 us -> 57.5 us  [the longest x1 56.7 us: shards(): pl.pallas_call(functools.partial(kernel, sizes), out_shape=shapes, in_spe...]
where the time goes in v2:
time: 58.4 us; the launch traced here: 58.3 us
  Pallas kernels  57.5 us (98%)
  between operations  0.82 us (1%)
    pallas_call x1, Pallas kernels, shards(): pl.pallas_call(functools.partial(kernel, sizes), out_shape=shapes, in_spe...  56.7 us

profile of v2, /device:TPU:0, one launch (start us, length us, event | category | flops | bytes accessed | tf_op | source)
XLA Modules:
  0.0 58.3 jit_solution(3534607068203242771)
XLA Ops:
  0.6 56.7 %tree_solve.1 = (f32[1,512,128]{2,1,0:T(8,128)S(1)}, f32[384,128]{1,0:T(8,128)S(1)}) custom-call(bf16[1,2,512,2048]{3,2,1,0:T(8,128)(2,1)} %factor_hbm.1, s32[1,16,16]{2,1,0:T(8,128)} %pattern_hbm.1, f32[1,512,2048]{2,1,0:T(8,128)} %inverse_hbm.1, bf16[1,1,512,1024]{3,2,1,0:T(8,128)(2,1)} %couple_hbm.1, s32[1,1024]{1,0:T(1,128)} %rows_hbm.1, ...), custom_call_target="tpu_custom_call" | custom-call | tf_op jit(solution)/shard_map/tree_solve/pallas_call | solution.py:583
  57.3 0.8 %publish.1 = (f32[1,512,128]{2,1,0:T(8,128)}, f32[384,128]{1,0:T(8,128)}) custom-call(f32[1,512,128]{2,1,0:T(8,128)S(1)} %get-tuple-element.4.x, f32[384,128]{1,0:T(8,128)S(1)} %get-tuple-element.5.root), custom_call_target="tpu_custom_call" | custom-call | tf_op jit(solution)/shard_map/publish/pallas_call | solution.py:594

commit v3 on v2

--- a/solution.py
+++ b/solution.py
@@ -125,6 +125,7 @@
     share = r_raw.shape[0]
     separator = r_raw.shape[1]
     tall, wide, steps = offsets(cols)
+    whole_lanes = share % 128 == 0
     col_y = lax.div(col, wide)
     col_x = lax.rem(col, wide)
 
@@ -181,69 +182,79 @@
             source, target, pair_snd.at[index], pair_rcv.at[index], device_id={"row": 1 - row}
         )
 
-    def to_col(source, target, slot, i):
+    def to_col(source, target, kind, slot, i):
         return pltpu.make_async_remote_copy(
-            source, target, col_snd.at[slot // SLOTS], col_rcv.at[slot, i], device_id={"col": ahead(i)}
+            source, target, col_snd.at[kind], col_rcv.at[slot], device_id={"col": ahead(i)}
         )
 
-    def to_other(source, target, slot, i):
+    def gather_slot(i):
+        return SLOTS + (2 if i == 0 else 0 if i == 1 else 1)
+
+    def to_other(source, target, i):
         return pltpu.make_async_remote_copy(
             source,
             target,
-            col_snd.at[slot // SLOTS],
-            col_rcv.at[slot, i],
+            col_snd.at[1],
+            col_rcv.at[gather_slot(i)],
             device_id={"row": 1 - row, "col": ahead(i)},
         )
 
-    def scatter(make, size, receive, segments, pieces):
-        pieces = divided(size, pieces)
-        segments = min(segments, pieces)
-        extent = size // segments
+    def arrived(slot, first, count, start, size):
+        block = part_snd.at[pl.ds(first, count), pl.ds(start, size)]
+        pltpu.make_async_remote_copy(
+            block, block, col_snd.at[0], col_rcv.at[slot], device_id={"row": 1 - row}
+        ).wait_recv()
+
+    def far_arrived(size):
+        arrived(SLOTS, 1, 1, 0, size)
+
+    def near_arrived(count, size):
+        arrived(SLOTS + 1, 0, count, 0, size)
+
+    def scatter(make, size, receive):
+        pieces = divided(size, SLOTS)
         fine = size // pieces
-        copies = []
-        for segment in range(segments):
-            rows = pl.ds(segment * extent, extent)
-            for i in range(1, cols):
-                value = make(i, ahead(i), segment * extent, extent)
-                part_snd[i, rows, :] = value.astype(BF16)
-            part_own[rows, :] = make(0, col, segment * extent, extent)
-            for piece in range(pieces // segments):
-                at = pl.ds(segment * extent + piece * fine, fine)
-                slot = len(copies)
-                sent = []
-                for i in range(1, cols):
-                    copy = to_col(part_snd.at[i, at], receive.at[i, at], slot, i)
-                    copy.start()
-                    sent.append(copy)
-                copies.append((at, sent))
-        return copies
-
-    def gathered(receive, at, sent):
-        for copy in sent:
-            copy.wait_recv()
+        spans = [pl.ds(piece * fine, fine) for piece in range(pieces)]
+        batches = [[(1, 0)]]
+        for piece in range(pieces):
+            batch = [(i, piece) for i in range(2, cols)] + [(0, piece)]
+            if piece + 1 < pieces:
+                batch.insert(0, (1, piece + 1))
+            batches.append(batch)
+        for batch in batches:
+            for i, piece in batch:
+                value = make(i, ahead(i), piece * fine, fine)
+                if i > 0:
+                    part_snd[i, spans[piece], :] = value.astype(BF16)
+                else:
+                    part_own[spans[piece], :] = value
+            for i, piece in batch:
+                if i > 0:
+                    at = spans[piece]
+                    to_col(part_snd.at[i, at], receive.at[i, at], 0, piece, i).start()
+        return [(at, piece, fine) for piece, at in enumerate(spans)]
+
+    def gathered(receive, at, slot, fine):
+        arrived(slot, 1, cols - 1, 0, fine)
         total = part_own[at, :]
         for i in range(1, cols):
             total = total + receive[i, at, :].astype(F32)
         return total
 
-    def share_out(target, slot):
-        copies = []
+    def share_out(target):
         for i in range(1, cols):
-            copy = to_col(target, target, slot, i)
-            copy.start()
-            copies.append(copy)
-        return copies
+            to_col(target, target, 1, gather_slot(i), i).start()
 
     def sent_out(kind, first, size):
         block = part_snd.at[pl.ds(first, cols - first), pl.ds(0, size)]
         pltpu.make_async_remote_copy(
-            block, block, col_snd.at[kind], col_rcv.at[0, 0], device_id={"row": 1 - row}
+            block, block, col_snd.at[kind], col_rcv.at[0], device_id={"row": 1 - row}
         ).wait_send()
 
     def sent_across():
         block = z_rcv.at[pl.ds(1, subs - 1)]
         pltpu.make_async_remote_copy(
-            block, block, z_ssem.at[0], z_rsem.at[0, 0], device_id={"row": 1 - row}
+            block, block, z_ssem.at[0], z_rsem.at[0], device_id={"row": 1 - row}
         ).wait_send()
 
     def finish(copies):
@@ -315,26 +326,24 @@
         root_whole.wait_recv()
         root_out[...] = root_keep[...]
         m_whole.wait_recv()
-        count = divided(width, 4)
-        fine = width // count
-        near = [0] + list(range(2, cols))
-        for group in (near, [1]):
-            for i in group:
-                for piece in range(count):
-                    at = pl.ds(piece * fine, fine)
-                    to_other(
-                        x_all.at[i, at], x_all.at[i, at], SLOTS + piece, i
-                    ).wait_recv()
+        near = list(range(2, cols))
+        for group in ([0], near, [1]):
+            if group is near:
+                near_arrived(cols - 2, width)
+            elif group[0] > 0:
+                far_arrived(width)
+            else:
+                arrived(SLOTS + 2, 0, 1, 0, width)
             total = y_keep[...]
             for i in group:
                 total = total - mm(m_raw[:, part(behind(i), width)], x_all[i])
-            if group is near:
+            if group[0] != 1:
                 y_keep[...] = total
             else:
                 w_pair[0:width, :] = paired(total)
-        sends = scatter(turned, width, back_rcv, 2, 4)
-        for at, sent in sends:
-            x_out[0, at, :] = gathered(back_rcv, at, sent)
+        sends = scatter(turned, width, back_rcv)
+        for at, slot, fine in sends:
+            x_out[0, at, :] = gathered(back_rcv, at, slot, fine)
         sent_out(0, 1, width)
         finish(y_parts + [mapped_whole])
 
@@ -365,7 +374,7 @@
         def a_rows(i, k, start, extent):
             return mm(m_turn[i, pl.ds(start, extent), :], y_low[...])
 
-        sends_a = scatter(a_rows, width, a_rcv, 2, 4)
+        sends_a = scatter(a_rows, width, a_rcv)
 
         def put(rows, value):
             y_keep[rows, :] = value
@@ -376,16 +385,16 @@
             copy.wait()
         for c in range(CHUNKS):
             apply_inverse(c, put)
-        sends_b = []
-        for at, sent in sends_a:
-            a_all[col, at, :] = gathered(a_rcv, at, sent).astype(BF16)
-            sends_b.append(share_out(a_all.at[col, at], SLOTS + len(sends_b)))
+        for at, slot, fine in sends_a:
+            a_all[col, at, :] = gathered(a_rcv, at, slot, fine).astype(BF16)
+            share_out(a_all.at[col, at])
         make_spread_turn()
-        for group in ([0] + list(range(2, cols)), [1]):
-            for i in group:
-                if i > 0:
-                    for sent in sends_b:
-                        sent[i - 1].wait_recv()
+        near = list(range(2, cols))
+        for group in ([0], near, [1]):
+            if group is near:
+                near_arrived(cols - 2, width)
+            elif group[0] > 0:
+                far_arrived(width)
             total = y_keep[...]
             for i in group:
                 k = behind(i)
@@ -400,7 +409,7 @@
             return mm(spread[place, :], y_low[...]) + mapped_rcv[place, :]
 
         sent_out(0, 1, width)
-        sends_c = scatter(separator_rows, share, s_rcv, 2, 4)
+        sends_c = scatter(separator_rows, share, s_rcv)
         get_r.wait()
         get_rr.wait()
         r_hi[...], r_lo[...] = halves(r_raw[...])
@@ -408,29 +417,33 @@
             ends = slice(first, first + step)
             rt_hi[ends, :], rt_lo[ends, :] = halves(r_raw[:, ends].T)
         sends_z = []
-        for piece, (at, sent) in enumerate(sends_c):
-            total = gathered(s_rcv, at, sent)
+        for piece, (at, slot, fine) in enumerate(sends_c):
+            total = gathered(s_rcv, at, slot, fine)
             part_own[at, :] = total
             z_snd[at, :] = total.astype(BF16)
-            copies = []
             for d in range(1, subs):
                 copy = pltpu.make_async_remote_copy(
                     z_snd.at[at],
                     z_rcv.at[d, at],
                     z_ssem.at[0],
-                    z_rsem.at[piece, d - 1],
+                    z_rsem.at[piece],
                     device_id={"sub": lax.rem(sub + d, subs)},
                 )
                 copy.start()
-                copies.append(copy)
-            sends_z.append((at, copies))
+            sends_z.append(at)
         turn_inverse()
         sent_out(1, 1, width)
-        sends_d = []
+        def root_block(i):
+            ends = part(behind(i), share)
+            right = rhs_hi[ends, :]
+            return mm(r_hi[:, ends], right) + mm(r_lo[:, ends], right)
+
         fine = share // len(sends_z)
-        for piece, (at, copies) in enumerate(sends_z):
-            for copy in copies:
-                copy.wait_recv()
+        for piece, at in enumerate(sends_z):
+            block = z_rcv.at[pl.ds(1, subs - 1), at]
+            pltpu.make_async_remote_copy(
+                block, block, z_ssem.at[0], z_rsem.at[piece], device_id={"row": 1 - row}
+            ).wait_recv()
             total = part_own[at, :]
             for d in range(1, subs):
                 total = total + z_rcv[d, at, :].astype(F32)
@@ -438,46 +451,67 @@
             place = pl.ds(pl.multiple_of(col * share + piece * fine, 16), fine)
             rhs_hi[place, :] = high
             rhs_lo[place, :] = low
-            sends_d.append(share_out(rhs_hi.at[place], SLOTS + piece))
-        own_half = mm(r_hi[...], rhs_lo[...])
-        part_own[0:share, :] = own_half
-        for sent in sends_d:
-            for copy in sent:
-                copy.wait_recv()
-        half = mm(r_hi[...], rhs_hi[...]) + mm(r_lo[...], rhs_hi[...])
-        w_pair[0:share, :] = paired(half + part_own[0:share, :])
+            share_out(rhs_hi.at[place])
+        if whole_lanes:
+            own = part(col, share)
+            part_own[0:share, :] = mm(r_hi[:, own], rhs_lo[own, :]) + root_block(0)
+            near_arrived(cols - 2, share)
+            near_total = part_own[0:share, :]
+            for i in range(2, cols):
+                near_total = near_total + root_block(i)
+            part_own[0:share, :] = near_total
+            far_arrived(share)
+            root_half = part_own[0:share, :] + root_block(1)
+        else:
+            part_own[0:share, :] = mm(r_hi[...], rhs_lo[...])
+            near_arrived(cols - 2, share)
+            far_arrived(share)
+            root_half = mm(r_hi[...], rhs_hi[...]) + mm(r_lo[...], rhs_hi[...])
+            root_half = root_half + part_own[0:share, :]
+        w_pair[0:share, :] = paired(root_half)
+
+        def coupled_block(i):
+            ends = part(behind(i), share)
+            return mm(spread_turn[:, ends], sep_low[ends, :])
 
         def root_rows(i, k, start, extent):
             place = pl.ds(pl.multiple_of(k * share + start, 16), extent)
             return mm_paired(rt_hi[place, :], rt_lo[place, :], w_pair[0:share, :])
 
         sent_out(0, 1, share)
-        sends_e = scatter(root_rows, share, t_rcv, 2, 2)
+        sends_e = scatter(root_rows, share, t_rcv)
         sent_out(1, 1, share)
-        sends_f = []
-        fine = share // len(sends_e)
-        for piece, (at, sent) in enumerate(sends_e):
-            total = gathered(t_rcv, at, sent)
+        for piece, (at, slot, fine) in enumerate(sends_e):
+            total = gathered(t_rcv, at, slot, fine)
             place = pl.ds(pl.multiple_of(col * share + piece * fine, 16), fine)
             sep_low[place, :] = total.astype(BF16)
-            sends_f.append(share_out(sep_low.at[place], SLOTS + piece))
+            share_out(sep_low.at[place])
             root_out[at, :] = total
             root_keep[at, :] = total
         root_whole.start()
-        for sent in sends_f:
-            for copy in sent:
-                copy.wait_recv()
-        sep_whole.start()
-        w_pair[0:width, :] = paired(y_keep[...] - mm(spread_turn[...], sep_low[...]))
+        if whole_lanes:
+            y_keep[...] = y_keep[...] - coupled_block(0)
+            near_arrived(cols - 2, share)
+            total = y_keep[...]
+            for i in range(2, cols):
+                total = total - coupled_block(i)
+            y_keep[...] = total
+            far_arrived(share)
+            sep_whole.start()
+            w_pair[0:width, :] = paired(y_keep[...] - coupled_block(1))
+        else:
+            near_arrived(cols - 2, share)
+            far_arrived(share)
+            sep_whole.start()
+            w_pair[0:width, :] = paired(y_keep[...] - mm(spread_turn[...], sep_low[...]))
         sent_out(0, 1, share)
-        sends_g = scatter(turned, width, back_rcv, 2, 4)
+        sends_g = scatter(turned, width, back_rcv)
         sent_out(1, 1, share)
-        for piece, (at, sent) in enumerate(sends_g):
-            total = gathered(back_rcv, at, sent)
+        for at, slot, fine in sends_g:
+            total = gathered(back_rcv, at, slot, fine)
             y_low[at, :] = total.astype(BF16)
             for i in list(range(1, cols)) + [0]:
-                copy = to_other(y_low.at[at], x_all.at[i, at], SLOTS + piece, i)
-                copy.start()
+                to_other(y_low.at[at], x_all.at[i, at], i).start()
             x_out[0, at, :] = total
         sent_across()
         sent_out(0, 1, width)
@@ -562,9 +596,9 @@
         DMA((4 + CHUNKS,)),
         DMA((4 + CHUNKS,)),
         DMA((2,)),
-        DMA((2 * SLOTS, cols)),
+        DMA((SLOTS + 3,)),
         DMA((1,)),
-        DMA((SLOTS, subs - 1)),
+        DMA((SLOTS,)),
     ]
     inputs = (
         factor_cols,

time: 58.4 us -> 55.1 us (0.943)
  Pallas kernels: 57.5 us -> 54.2 us
    pallas_call x1, Pallas kernels: 56.7 us -> 53.4 us  [shards(): pl.pallas_call(functools.partial(kernel, sizes), out_shape=shapes, in_spe...]
where the time goes in v3:
time: 55.1 us; the launch traced here: 55 us
  Pallas kernels  54.2 us (98%)
  between operations  0.82 us (1%)
    pallas_call x1, Pallas kernels, shards(): pl.pallas_call(functools.partial(kernel, sizes), out_shape=shapes, in_spe...  53.4 us

profile of v3, /device:TPU:0, one launch (start us, length us, event | category | flops | bytes accessed | tf_op | source)
XLA Modules:
  0.0 55.0 jit_solution(1843941297752886892)
XLA Ops:
  0.6 53.4 %tree_solve.1 = (f32[1,512,128]{2,1,0:T(8,128)S(1)}, f32[384,128]{1,0:T(8,128)S(1)}) custom-call(bf16[1,2,512,2048]{3,2,1,0:T(8,128)(2,1)} %factor_hbm.1, s32[1,16,16]{2,1,0:T(8,128)} %pattern_hbm.1, f32[1,512,2048]{2,1,0:T(8,128)} %inverse_hbm.1, bf16[1,1,512,1024]{3,2,1,0:T(8,128)(2,1)} %couple_hbm.1, s32[1,1024]{1,0:T(1,128)} %rows_hbm.1, ...), custom_call_target="tpu_custom_call" | custom-call | tf_op jit(solution)/shard_map/tree_solve/pallas_call | solution.py:617
  54.0 0.8 %publish.1 = (f32[1,512,128]{2,1,0:T(8,128)}, f32[384,128]{1,0:T(8,128)}) custom-call(f32[1,512,128]{2,1,0:T(8,128)S(1)} %get-tuple-element.4.x, f32[384,128]{1,0:T(8,128)S(1)} %get-tuple-element.5.root), custom_call_target="tpu_custom_call" | custom-call | tf_op jit(solution)/shard_map/publish/pallas_call | solution.py:628

commit v4 on v3

--- a/solution.py
+++ b/solution.py
@@ -11,7 +11,8 @@
 F32 = jnp.float32
 BF16 = jnp.bfloat16
 CHUNKS = 2
-SLOTS = 4
+BLOCKS = 4
+SLOTS = 8
 
 
 def mm(a, b):
@@ -32,10 +33,31 @@
     return jnp.concatenate(halves(x), axis=1)
 
 
+def stacked(blocks, right):
+    tall = mm(jnp.concatenate(blocks, axis=0), right) if len(blocks) > 1 else mm(blocks[0], right)
+    values, at = [], 0
+    for block in blocks:
+        values.append(tall[at : at + block.shape[0], :])
+        at += block.shape[0]
+    return values
+
+
+def mm_split(high, low, right):
+    first, second = stacked([high, low], right)
+    return first + second
+
+
+def folded(both):
+    sources = both.shape[1] // 2
+    return both[:, :sources] + both[:, sources:]
+
+
 def mm_paired(high, low, pair):
-    both = mm(high, pair) + mm(low, pair)
-    sources = pair.shape[1] // 2
-    return both[:, :sources] + both[:, sources:]
+    return folded(mm_split(high, low, pair))
+
+
+def mm_apart(high, low, pair):
+    return folded(mm(high, pair) + mm(low, pair))
 
 
 def divided(size, most):
@@ -160,7 +182,7 @@
 
     @pl.when(row != 0)
     def _():
-        for copy in [get_p, get_m, get_n, get_c, get_b] + get_e + [get_r, get_rr]:
+        for copy in [get_p, get_m, get_n, get_c]:
             copy.start()
 
     barrier = pltpu.get_barrier_semaphore()
@@ -212,27 +234,32 @@
         arrived(SLOTS + 1, 0, count, 0, size)
 
     def scatter(make, size, receive):
+        blocks = divided(size, BLOCKS)
         pieces = divided(size, SLOTS)
+        tallest = size // blocks
         fine = size // pieces
-        spans = [pl.ds(piece * fine, fine) for piece in range(pieces)]
+        each = pieces // blocks
         batches = [[(1, 0)]]
-        for piece in range(pieces):
-            batch = [(i, piece) for i in range(2, cols)] + [(0, piece)]
-            if piece + 1 < pieces:
-                batch.insert(0, (1, piece + 1))
+        for block in range(blocks):
+            batch = [(i, block) for i in range(2, cols)] + [(0, block)]
+            if block + 1 < blocks:
+                batch.insert(0, (1, block + 1))
             batches.append(batch)
         for batch in batches:
-            for i, piece in batch:
-                value = make(i, ahead(i), piece * fine, fine)
+            values = make([(i, block * tallest, tallest) for i, block in batch])
+            for (i, block), value in zip(batch, values):
+                rows = pl.ds(block * tallest, tallest)
                 if i > 0:
-                    part_snd[i, spans[piece], :] = value.astype(BF16)
+                    part_snd[i, rows, :] = value.astype(BF16)
                 else:
-                    part_own[spans[piece], :] = value
-            for i, piece in batch:
-                if i > 0:
-                    at = spans[piece]
-                    to_col(part_snd.at[i, at], receive.at[i, at], 0, piece, i).start()
-        return [(at, piece, fine) for piece, at in enumerate(spans)]
+                    part_own[rows, :] = value
+            for turn in range(each):
+                for i, block in batch:
+                    if i > 0:
+                        piece = block * each + turn
+                        at = pl.ds(piece * fine, fine)
+                        to_col(part_snd.at[i, at], receive.at[i, at], 0, piece, i).start()
+        return [(pl.ds(piece * fine, fine), piece, fine) for piece in range(pieces)]
 
     def gathered(receive, at, slot, fine):
         arrived(slot, 1, cols - 1, 0, fine)
@@ -287,9 +314,12 @@
         for first in range(0, separator, step):
             spread_turn[:, first : first + step] = mm_nt(c_raw[...], hits(first)).astype(BF16)
 
-    def turned(i, k, start, extent):
-        rows = pl.ds(start, extent)
-        return mm_paired(et_hi[i, rows, :], et_lo[i, rows, :], w_pair[0:width, :])
+    def turned(blocks):
+        values = []
+        for i, start, size in blocks:
+            rows = pl.ds(start, size)
+            values.append(mm_paired(et_hi[i, rows, :], et_lo[i, rows, :], w_pair[0:width, :]))
+        return values
 
     y_parts = []
     for c in range(CHUNKS):
@@ -308,12 +338,13 @@
 
         get_b.wait()
         b_pair[...] = paired(b_raw[...])
+        for copy in get_e:
+            copy.wait()
         for c in range(CHUNKS):
-            get_e[c].wait()
             apply_inverse(c, put)
-            if c == 0:
-                greet()
-            y_parts[c].start()
+        greet()
+        for copy in y_parts:
+            copy.start()
         get_c.wait()
         get_n.wait()
         make_spread()
@@ -360,6 +391,8 @@
                 kept = m_raw[at : at + high_rows, ends].astype(F32) * present
                 m_raw[at : at + high_rows, ends] = kept.astype(BF16)
         greet()
+        for copy in [get_b] + get_e + [get_r, get_rr]:
+            copy.start()
         m_whole.start()
         for i in range(cols):
             block = m_raw[:, part(ahead(i), width)]
@@ -371,8 +404,9 @@
         for copy in y_parts:
             copy.wait_recv()
 
-        def a_rows(i, k, start, extent):
-            return mm(m_turn[i, pl.ds(start, extent), :], y_low[...])
+        def a_rows(blocks):
+            rows = [m_turn[i, pl.ds(start, size), :] for i, start, size in blocks]
+            return [mm(block, y_low[...]) for block in rows]
 
         sends_a = scatter(a_rows, width, a_rcv)
 
@@ -399,14 +433,18 @@
             for i in group:
                 k = behind(i)
                 ends = part(k, width)
-                total = total - (mm(e_hi[:, ends], a_all[k]) + mm(e_lo[:, ends], a_all[k]))
+                total = total - mm_split(e_hi[:, ends], e_lo[:, ends], a_all[k])
             y_keep[...] = total
         y_low[...] = y_keep[...].astype(BF16)
         mapped_whole.wait_recv()
 
-        def separator_rows(i, k, start, extent):
-            place = pl.ds(pl.multiple_of(k * share + start, 16), extent)
-            return mm(spread[place, :], y_low[...]) + mapped_rcv[place, :]
+        def shared(i, start, size):
+            return pl.ds(pl.multiple_of(ahead(i) * share + start, 16), size)
+
+        def separator_rows(blocks):
+            places = [shared(*block) for block in blocks]
+            values = [mm(spread[place, :], y_low[...]) for place in places]
+            return [value + mapped_rcv[place, :] for place, value in zip(places, values)]
 
         sent_out(0, 1, width)
         sends_c = scatter(separator_rows, share, s_rcv)
@@ -436,7 +474,7 @@
         def root_block(i):
             ends = part(behind(i), share)
             right = rhs_hi[ends, :]
-            return mm(r_hi[:, ends], right) + mm(r_lo[:, ends], right)
+            return mm_split(r_hi[:, ends], r_lo[:, ends], right)
 
         fine = share // len(sends_z)
         for piece, at in enumerate(sends_z):
@@ -466,7 +504,7 @@
             part_own[0:share, :] = mm(r_hi[...], rhs_lo[...])
             near_arrived(cols - 2, share)
             far_arrived(share)
-            root_half = mm(r_hi[...], rhs_hi[...]) + mm(r_lo[...], rhs_hi[...])
+            root_half = mm_split(r_hi[...], r_lo[...], rhs_hi[...])
             root_half = root_half + part_own[0:share, :]
         w_pair[0:share, :] = paired(root_half)
 
@@ -474,9 +512,10 @@
             ends = part(behind(i), share)
             return mm(spread_turn[:, ends], sep_low[ends, :])
 
-        def root_rows(i, k, start, extent):
-            place = pl.ds(pl.multiple_of(k * share + start, 16), extent)
-            return mm_paired(rt_hi[place, :], rt_lo[place, :], w_pair[0:share, :])
+        def root_rows(blocks):
+            places = [shared(*block) for block in blocks]
+            pair = w_pair[0:share, :]
+            return [mm_paired(rt_hi[place, :], rt_lo[place, :], pair) for place in places]
 
         sent_out(0, 1, share)
         sends_e = scatter(root_rows, share, t_rcv)

time: 55.1 us -> 54.2 us (0.984)
  Pallas kernels: 54.2 us -> 53.2 us
    pallas_call x1, Pallas kernels: 53.4 us -> 52.4 us  [shards(): pl.pallas_call(functools.partial(kernel, sizes), out_shape=shapes, in_spe...]
where the time goes in v4:
time: 54.2 us; the launch traced here: 54 us
  Pallas kernels  53.2 us (98%)
  between operations  0.82 us (2%)
    pallas_call x1, Pallas kernels, shards(): pl.pallas_call(functools.partial(kernel, sizes), out_shape=shapes, in_spe...  52.4 us

profile of v4, /device:TPU:0, one launch (start us, length us, event | category | flops | bytes accessed | tf_op | source)
XLA Modules:
  0.0 54.0 jit_solution(5543094280658158464)
XLA Ops:
  0.6 52.4 %tree_solve.1 = (f32[1,512,128]{2,1,0:T(8,128)S(1)}, f32[384,128]{1,0:T(8,128)S(1)}) custom-call(bf16[1,2,512,2048]{3,2,1,0:T(8,128)(2,1)} %factor_hbm.1, s32[1,16,16]{2,1,0:T(8,128)} %pattern_hbm.1, f32[1,512,2048]{2,1,0:T(8,128)} %inverse_hbm.1, bf16[1,1,512,1024]{3,2,1,0:T(8,128)(2,1)} %couple_hbm.1, s32[1,1024]{1,0:T(1,128)} %rows_hbm.1, ...), custom_call_target="tpu_custom_call" | custom-call | tf_op jit(solution)/shard_map/tree_solve/pallas_call | solution.py:656
  53.1 0.8 %publish.1 = (f32[1,512,128]{2,1,0:T(8,128)}, f32[384,128]{1,0:T(8,128)}) custom-call(f32[1,512,128]{2,1,0:T(8,128)S(1)} %get-tuple-element.4.x, f32[384,128]{1,0:T(8,128)S(1)} %get-tuple-element.5.root), custom_call_target="tpu_custom_call" | custom-call | tf_op jit(solution)/shard_map/publish/pallas_call | solution.py:667

commit v5 on v4

--- a/solution.py
+++ b/solution.py
@@ -417,12 +417,12 @@
         b_pair[...] = paired(b_raw[...])
         for copy in get_e:
             copy.wait()
-        for c in range(CHUNKS):
-            apply_inverse(c, put)
+        apply_inverse(0, put)
         for at, slot, fine in sends_a:
             a_all[col, at, :] = gathered(a_rcv, at, slot, fine).astype(BF16)
             share_out(a_all.at[col, at])
-        make_spread_turn()
+        for c in range(1, CHUNKS):
+            apply_inverse(c, put)
         near = list(range(2, cols))
         for group in ([0], near, [1]):
             if group is near:
@@ -459,7 +459,7 @@
             total = gathered(s_rcv, at, slot, fine)
             part_own[at, :] = total
             z_snd[at, :] = total.astype(BF16)
-            for d in range(1, subs):
+            for d in sorted(range(1, subs), key=lambda d: -min(d, subs - d)):
                 copy = pltpu.make_async_remote_copy(
                     z_snd.at[at],
                     z_rcv.at[d, at],
@@ -469,7 +469,7 @@
                 )
                 copy.start()
             sends_z.append(at)
-        turn_inverse()
+        make_spread_turn()
         sent_out(1, 1, width)
         def root_block(i):
             ends = part(behind(i), share)
@@ -493,6 +493,7 @@
         if whole_lanes:
             own = part(col, share)
             part_own[0:share, :] = mm(r_hi[:, own], rhs_lo[own, :]) + root_block(0)
+            turn_inverse()
             near_arrived(cols - 2, share)
             near_total = part_own[0:share, :]
             for i in range(2, cols):
@@ -502,6 +503,7 @@
             root_half = part_own[0:share, :] + root_block(1)
         else:
             part_own[0:share, :] = mm(r_hi[...], rhs_lo[...])
+            turn_inverse()
             near_arrived(cols - 2, share)
             far_arrived(share)
             root_half = mm_split(r_hi[...], r_lo[...], rhs_hi[...])

time: 54.2 us -> 54.1 us (level)
  no operation moved by 1% of the time
where the time goes in v5:
time: 54.1 us; the launch traced here: 54 us
  Pallas kernels  53.2 us (98%)
  between operations  0.82 us (2%)
    pallas_call x1, Pallas kernels, shards(): pl.pallas_call(functools.partial(kernel, sizes), out_shape=shapes, in_spe...  52.4 us

profile of v5, /device:TPU:0, one launch (start us, length us, event | category | flops | bytes accessed | tf_op | source)
XLA Modules:
  0.0 54.0 jit_solution(14309604823821881877)
XLA Ops:
  0.6 52.4 %tree_solve.1 = (f32[1,512,128]{2,1,0:T(8,128)S(1)}, f32[384,128]{1,0:T(8,128)S(1)}) custom-call(bf16[1,2,512,2048]{3,2,1,0:T(8,128)(2,1)} %factor_hbm.1, s32[1,16,16]{2,1,0:T(8,128)} %pattern_hbm.1, f32[1,512,2048]{2,1,0:T(8,128)} %inverse_hbm.1, bf16[1,1,512,1024]{3,2,1,0:T(8,128)(2,1)} %couple_hbm.1, s32[1,1024]{1,0:T(1,128)} %rows_hbm.1, ...), custom_call_target="tpu_custom_call" | custom-call | tf_op jit(solution)/shard_map/tree_solve/pallas_call | solution.py:658
  53.0 0.8 %publish.1 = (f32[1,512,128]{2,1,0:T(8,128)}, f32[384,128]{1,0:T(8,128)}) custom-call(f32[1,512,128]{2,1,0:T(8,128)S(1)} %get-tuple-element.4.x, f32[384,128]{1,0:T(8,128)S(1)} %get-tuple-element.5.root), custom_call_target="tpu_custom_call" | custom-call | tf_op jit(solution)/shard_map/publish/pallas_call | solution.py:669
